TPU v7x, 32 devices: a whole 2x2x4 slice. The times are simulated.
32 devices in a mesh: wide: 16 (over z, y, core), narrow: 2 (over x).
Axes of the slice: x: 2, y: 2, z: 4, core: 2. Of those that a mesh axis runs over, the one named last changes fastest.
Arguments:
- inputs: bfloat16 [18464, 1024], P('wide', 'narrow'), may hold values from -6 to 6
- counts: int32 [16], P('wide'), may hold values from 1 to 2, as said below
- ln1_gain: float32 [1024], P('narrow'), may hold values from 0.5 to 1.5
- ln1_bias: float32 [1024], P('narrow'), may hold values from -3 to 3
- w_qkv: bfloat16 [1024, 3072], P('wide', 'narrow'), may hold values from -2 to 2
- qv_bias: float32 [2048], P('narrow'), may hold values from -3 to 3
- w_proj: bfloat16 [1024, 1024], P('narrow', 'wide'), may hold values from -1.5 to 1.5
- proj_bias: float32 [1024], P('narrow'), may hold values from -3 to 3
- ln2_gain: float32 [1024], P('narrow'), may hold values from 0.5 to 1.5
- ln2_bias: float32 [1024], P('narrow'), may hold values from -3 to 3
- w_fc1: bfloat16 [1024, 4096], P('wide', 'narrow'), may hold values from -0.1875 to 0.1875
- fc1_bias: float32 [4096], P('narrow'), may hold values from -3 to 3
- w_fc2: bfloat16 [4096, 1024], P('narrow', 'wide'), may hold values from -0.09375 to 0.09375
- fc2_bias: float32 [1024], P('narrow'), may hold values from -3 to 3
- cotangent: bfloat16 [18464, 1024], P('wide', 'narrow'), may hold values from -6 to 6
Outputs:
- output: bfloat16 [18464, 1024], P('wide', 'narrow')
- grad_in: bfloat16 [18464, 1024], P('wide', 'narrow')
- grad_ln1_gain: float32 [1024], P('narrow')
- grad_ln1_bias: float32 [1024], P('narrow')
- grad_w_qkv: float32 [1024, 3072], P('wide', 'narrow')
- grad_qv_bias: float32 [2048], P('narrow')
- grad_w_proj: float32 [1024, 1024], P('narrow', 'wide')
- grad_proj_bias: float32 [1024], P('narrow')
- grad_ln2_gain: float32 [1024], P('narrow')
- grad_ln2_bias: float32 [1024], P('narrow')
- grad_w_fc1: float32 [1024, 4096], P('wide', 'narrow')
- grad_fc1_bias: float32 [4096], P('narrow')
- grad_w_fc2: float32 [4096, 1024], P('narrow', 'wide')
- grad_fc2_bias: float32 [1024], P('narrow')
Inputs may be any that keep to these rules, and one draw needn't show every extreme that they name: `counts`: each group's images fill its first slots; some group holds 2 images and some holds 1.
All inputs are finite; a program needn't handle non-finite values.
Results may differ from a plain program's by a relative error of at most 0.015.
The roundings to bfloat16 on the way count: a program that leaves them out, or rounds other values in their place, can miss the bound.
Values may be sent and summed in bfloat16 or wider, within the bound.
A program may use at most 192 MiB of HBM per device.

v0:
```python
import math

import jax
import jax.numpy as jnp
from jax import lax
from jax.sharding import PartitionSpec as P

DH = 64
SEQ = 577


norm_eps = 1e-06


def dot_trans_right(left_mat, right_mat):
    return lax.dot_general(
        left_mat, right_mat, (((1,), (1,)), ((), ())), preferred_element_type=jnp.float32
    )


def dot_trans_left(left_mat, right_mat):
    return lax.dot_general(
        left_mat, right_mat, (((0,), (0,)), ((), ())), preferred_element_type=jnp.float32
    )


def widen_rows(piece_rows):
    return lax.all_gather(piece_rows, "narrow", axis=1, tiled=True)


def narrow_sum(partial_rows):
    return lax.psum_scatter(partial_rows, "narrow", scatter_dimension=1, tiled=True)


def normal_cdf(values_in):
    return 0.5 * (1.0 + lax.erf(values_in * (1.0 / math.sqrt(2.0))))


def gelu_exact(values_in):
    return values_in * normal_cdf(values_in)


def gelu_slope(values_in):
    return normal_cdf(values_in) + values_in * jnp.exp(-0.5 * values_in * values_in) * (
        1.0 / math.sqrt(2.0 * math.pi)
    )


def norm_forward(local_rows, gain_vec, shift_vec, feature_width):
    totals = lax.psum(
        (jnp.sum(local_rows, axis=1), jnp.sum(local_rows * local_rows, axis=1)), "narrow"
    )
    center = totals[0] / feature_width
    spread = totals[1] / feature_width - center * center
    inv_std = lax.rsqrt(spread + norm_eps)
    normalized = (local_rows - center[:, None]) * inv_std[:, None]
    return (normalized, inv_std, (normalized * gain_vec + shift_vec).astype(jnp.bfloat16))


def norm_backward(incoming, normalized, inv_std, gain_vec, feature_width):
    scaled = incoming * gain_vec
    totals = lax.psum((jnp.sum(scaled, axis=1), jnp.sum(scaled * normalized, axis=1)), "narrow")
    back = inv_std[:, None] * (
        scaled
        - totals[0][:, None] / feature_width
        - normalized * (totals[1][:, None] / feature_width)
    )
    return (back, jnp.sum(incoming * normalized, axis=0), jnp.sum(incoming, axis=0))


def attend(queries, key_rows, value_rows, score_scale):
    scores = (
        jnp.einsum("sqhd,skhd->shqk", queries, key_rows, preferred_element_type=jnp.float32)
        * score_scale
    )
    row_max = jnp.max(scores, axis=-1, keepdims=True)
    exp_scores = jnp.exp(scores - row_max)
    row_total = jnp.sum(exp_scores, axis=-1, keepdims=True)
    probs_bf = (exp_scores / row_total).astype(jnp.bfloat16)
    mixed_out = jnp.einsum(
        "shqk,skhd->sqhd", probs_bf, value_rows, preferred_element_type=jnp.float32
    )
    return (mixed_out.astype(jnp.bfloat16), (row_max + jnp.log(row_total))[..., 0])


def attend_backward(queries, key_rows, value_rows, mixed_out, logsum, d_mixed, score_scale):
    scores = (
        jnp.einsum("sqhd,skhd->shqk", queries, key_rows, preferred_element_type=jnp.float32)
        * score_scale
    )
    probs_re = jnp.exp(scores - logsum[..., None])
    d_probs = jnp.einsum("sqhd,skhd->shqk", d_mixed, value_rows, preferred_element_type=jnp.float32)
    row_delta = jnp.sum(d_mixed.astype(jnp.float32) * mixed_out.astype(jnp.float32), axis=-1)
    row_delta = jnp.transpose(row_delta, (0, 2, 1))
    d_scores = (probs_re * (d_probs - row_delta[..., None])).astype(jnp.bfloat16)
    d_query = (
        jnp.einsum("shqk,skhd->sqhd", d_scores, key_rows, preferred_element_type=jnp.float32)
        * score_scale
    )
    d_keys = (
        jnp.einsum("shqk,sqhd->skhd", d_scores, queries, preferred_element_type=jnp.float32)
        * score_scale
    )
    d_values = jnp.einsum(
        "shqk,sqhd->skhd",
        probs_re.astype(jnp.bfloat16),
        d_mixed,
        preferred_element_type=jnp.float32,
    )
    return (d_query, d_keys, d_values)


def shards(
    inputs,
    counts,
    ln1_gain,
    ln1_bias,
    w_qkv,
    qv_bias,
    w_proj,
    proj_bias,
    ln2_gain,
    ln2_bias,
    w_fc1,
    fc1_bias,
    w_fc2,
    fc2_bias,
    cotangent,
):
    row_count = inputs.shape[0]
    feature_width = float(inputs.shape[1] * lax.axis_size("narrow"))
    slot_count = row_count // SEQ
    head_count = w_qkv.shape[1] // (3 * DH)
    score_scale = 1.0 / math.sqrt(DH)
    slot_of_row = lax.broadcasted_iota(jnp.int32, (row_count, 1), 0) // SEQ
    live_rows = (slot_of_row < counts[0]).astype(jnp.float32)
    wqkv_full, wfc1_full = (
        lax.all_gather(w_qkv, "wide", axis=0, tiled=True),
        lax.all_gather(w_fc1, "wide", axis=0, tiled=True),
    )
    wproj_full, wfc2_full = (
        lax.all_gather(w_proj, "wide", axis=1, tiled=True),
        lax.all_gather(w_fc2, "wide", axis=1, tiled=True),
    )
    resid = inputs.astype(jnp.float32)
    hat_one, inv_one, normed1 = norm_forward(resid, ln1_gain, ln1_bias, feature_width)
    normed1_full = widen_rows(normed1)
    bias_qv = qv_bias.reshape(head_count, 2, DH)
    bias_full = jnp.stack([bias_qv[:, 0], jnp.zeros_like(bias_qv[:, 0]), bias_qv[:, 1]], axis=1)
    qkv_rows = (
        jnp.dot(normed1_full, wqkv_full, preferred_element_type=jnp.float32).reshape(
            row_count, head_count, 3, DH
        )
        + bias_full
    )
    qkv_rows = qkv_rows.astype(jnp.bfloat16).reshape(slot_count, SEQ, head_count, 3, DH)
    queries = qkv_rows[:, :, :, 0]
    key_rows = qkv_rows[:, :, :, 1]
    value_rows = qkv_rows[:, :, :, 2]
    mixed_out, logsum = attend(queries, key_rows, value_rows, score_scale)
    mixed_rows = mixed_out.reshape(row_count, head_count * DH)
    attn_out = (
        narrow_sum(jnp.dot(mixed_rows, wproj_full, preferred_element_type=jnp.float32)) + proj_bias
    )
    resid_mid = resid + live_rows * attn_out
    hat_two, inv_two, normed2 = norm_forward(resid_mid, ln2_gain, ln2_bias, feature_width)
    normed2_full = widen_rows(normed2)
    inner_pre = jnp.dot(normed2_full, wfc1_full, preferred_element_type=jnp.float32) + fc1_bias
    activation = gelu_exact(inner_pre).astype(jnp.bfloat16)
    mlp_out = (
        narrow_sum(jnp.dot(activation, wfc2_full, preferred_element_type=jnp.float32)) + fc2_bias
    )
    output = (resid_mid + live_rows * mlp_out).astype(jnp.bfloat16)
    wqkv_back, wfc1_back = (wqkv_full, wfc1_full)
    wproj_back, wfc2_back = (wproj_full, wfc2_full)
    grad_out = cotangent.astype(jnp.float32)
    masked2 = live_rows * grad_out
    sent2 = widen_rows(masked2.astype(jnp.bfloat16))
    grad_w_fc2 = dot_trans_left(activation, sent2)
    d_inner = dot_trans_right(sent2, wfc2_back) * gelu_slope(inner_pre)
    d_inner_b = d_inner.astype(jnp.bfloat16)
    grad_w_fc1 = dot_trans_left(normed2_full, d_inner_b)
    d_norm2 = narrow_sum(dot_trans_right(d_inner_b, wfc1_back))
    back_two, grad_ln2_gain, grad_ln2_bias = norm_backward(
        d_norm2, hat_two, inv_two, ln2_gain, feature_width
    )
    d_mid = grad_out + back_two
    masked1 = live_rows * d_mid
    sent1 = widen_rows(masked1.astype(jnp.bfloat16))
    grad_w_proj = dot_trans_left(mixed_rows, sent1)
    d_mixed = (
        dot_trans_right(sent1, wproj_back)
        .astype(jnp.bfloat16)
        .reshape(slot_count, SEQ, head_count, DH)
    )
    d_query, d_keys, d_values = attend_backward(
        queries, key_rows, value_rows, mixed_out, logsum, d_mixed, score_scale
    )
    d_qkv = jnp.stack([d_query, d_keys, d_values], axis=3).reshape(row_count, head_count * 3 * DH)
    grad_qv_bias = jnp.stack(
        [jnp.sum(d_query, axis=(0, 1)), jnp.sum(d_values, axis=(0, 1))], axis=1
    ).reshape(head_count * 2 * DH)
    d_qkv_b = d_qkv.astype(jnp.bfloat16)
    grad_w_qkv = dot_trans_left(normed1_full, d_qkv_b)
    d_norm1 = narrow_sum(dot_trans_right(d_qkv_b, wqkv_back))
    back_one, grad_ln1_gain, grad_ln1_bias = norm_backward(
        d_norm1, hat_one, inv_one, ln1_gain, feature_width
    )
    grad_in = (d_mid + back_one).astype(jnp.bfloat16)
    grad_w_qkv, grad_w_fc1 = (
        lax.psum_scatter(
            grad_w_qkv.astype(jnp.bfloat16), "wide", scatter_dimension=0, tiled=True
        ).astype(jnp.float32),
        lax.psum_scatter(
            grad_w_fc1.astype(jnp.bfloat16), "wide", scatter_dimension=0, tiled=True
        ).astype(jnp.float32),
    )
    grad_w_proj, grad_w_fc2 = (
        lax.psum_scatter(
            grad_w_proj.astype(jnp.bfloat16), "wide", scatter_dimension=1, tiled=True
        ).astype(jnp.float32),
        lax.psum_scatter(
            grad_w_fc2.astype(jnp.bfloat16), "wide", scatter_dimension=1, tiled=True
        ).astype(jnp.float32),
    )
    summed = lax.psum(
        (
            grad_ln1_gain,
            grad_ln1_bias,
            grad_qv_bias,
            jnp.sum(masked1, axis=0),
            grad_ln2_gain,
            grad_ln2_bias,
            jnp.sum(d_inner, axis=0),
            jnp.sum(masked2, axis=0),
        ),
        "wide",
    )
    return (
        output,
        grad_in,
        summed[0],
        summed[1],
        grad_w_qkv,
        summed[2],
        grad_w_proj,
        summed[3],
        summed[4],
        summed[5],
        grad_w_fc1,
        summed[6],
        grad_w_fc2,
        summed[7],
    )


def solution(mesh):
    return jax.shard_map(
        shards,
        mesh=mesh,
        in_specs=(
            P("wide", "narrow"),
            P("wide"),
            P("narrow"),
            P("narrow"),
            P("wide", "narrow"),
            P("narrow"),
            P("narrow", "wide"),
            P("narrow"),
            P("narrow"),
            P("narrow"),
            P("wide", "narrow"),
            P("narrow"),
            P("narrow", "wide"),
            P("narrow"),
            P("wide", "narrow"),
        ),
        out_specs=(
            P("wide", "narrow"),
            P("wide", "narrow"),
            P("narrow"),
            P("narrow"),
            P("wide", "narrow"),
            P("narrow"),
            P("narrow", "wide"),
            P("narrow"),
            P("narrow"),
            P("narrow"),
            P("wide", "narrow"),
            P("narrow"),
            P("narrow", "wide"),
            P("narrow"),
        ),
        check_vma=False,
    )
```

profile of v0, /device:TPU:0, one launch (start us, length us, event | category | flops | bytes accessed | tf_op | source)
XLA Modules:
  0.0 1020.4 jit_solution(15430434548551709265)
XLA Ops:
  23.8 34.9 %all-gather.9.cloned.1.call-done = bf16[1154,1024]{1,0:T(8,128)(2,1)} async-done(((bf16[1154,512]{1,0:T(8,128)(2,1)}), bf16[1154,1024]{1,0:T(8,128)(2,1)}) %all-gather.9.cloned.1.call-update) | async-done | bytes 2363408 | tf_op jit(solution)/shard_map/all_gather | solution.py:28
  58.7 47.8 %all-gather.11.cloned.1.call-done = bf16[1024,1536]{1,0:T(8,128)(2,1)} async-done(((bf16[64,1536]{1,0:T(8,128)(2,1)}), bf16[1024,1536]{1,0:T(8,128)(2,1)}) %all-gather.11.cloned.1.call-update) | async-done | bytes 3145744 | tf_op jit(solution)/shard_map/all_gather | solution.py:138
  116.4 11.3 %reshape.105 = f32[2,577,8,3,64]{1,0,4,3,2:T(2,128)} reshape(f32[1154,1536]{0,1:T(8,128)} %fusion.48) | data formatting | bytes 14180352 | tf_op jit(solution)/shard_map/reshape | solution.py:151
  131.5 10.1 multiply_reduce_fusion
  141.6 10.4 %fusion = f32[2,8,577]{2,1,0:T(8,128)S(1)} fusion(f32[2,8,577,577]{2,3,1,0:T(8,128)} %get-tuple-element.55, f32[2,8,577]{2,1,0:T(8,128)S(1)} %get-tuple-element.54), kind=kLoop, calls=%fused_computation.4 | loop fusion | flops 15971360 | bytes 21381312 | tf_op jit(solution)/shard_map/reduce_sum | solution.py:78
  152.0 10.6 %fusion.33 = bf16[2,577,8,64]{1,3,2,0:T(8,128)(2,1)S(1)} fusion(f32[2,8,577,577]{2,3,1,0:T(8,128)} %get-tuple-element.55, f32[2,8,577]{2,1,0:T(8,128)S(1)} %fusion, f32[2,8,577]{2,1,0:T(8,128)S(1)} %get-tuple-element.54, bf16[2,577,8,3,64]{1,4,2,0,3:T(8,128)(2,1)S(1)} %fusion.11), kind=kOutput, calls=%fused_computation.71 | convolution fusion | flops 703736896 | bytes 23881792 | tf_op jit(solution)/shard_map/shqk,skhd->sqhd/dot_general | solution.py:80
  173.0 57.6 %reduce-scatter.9.cloned.1.call-done = f32[1154,512]{1,0:T(8,128)} async-done(((f32[1154,1024]{1,0:T(8,128)}), f32[1154,512]{1,0:T(8,128)}) %reduce-scatter.9.cloned.1.call-update) | async-done | bytes 2363408 | tf_op jit(solution)/shard_map/reduce_scatter | solution.py:32
  244.6 38.5 %all-gather.17.cloned.1.call-done = bf16[1024,2048]{1,0:T(8,128)(2,1)} async-done(((bf16[64,2048]{1,0:T(8,128)(2,1)}), bf16[1024,2048]{1,0:T(8,128)(2,1)}) %all-gather.17.cloned.1.call-update) | async-done | bytes 4194320 | tf_op jit(solution)/shard_map/all_gather | solution.py:139
  283.1 36.8 %all-gather.15.cloned.1.call-done = bf16[1154,1024]{1,0:T(8,128)(2,1)} async-done(((bf16[1154,512]{1,0:T(8,128)(2,1)}), bf16[1154,1024]{1,0:T(8,128)(2,1)}) %all-gather.15.cloned.1.call-update) | async-done | bytes 2363408 | tf_op jit(solution)/shard_map/all_gather | solution.py:28
  319.9 11.6 %multiply_convert_fusion.1 = (bf16[1154,2048]{1,0:T(8,128)(2,1)}, f32[1154,2048]{1,0:T(8,128)}) fusion(f32[2048]{0:T(1024)S(1)} %copy-done.25, bf16[1154,1024]{1,0:T(8,128)(2,1)} %all-gather.15.cloned.1.call-done, bf16[1024,2048]{1,0:T(8,128)(2,1)} %all-gather.17.cloned.1.call-done), kind=kOutput, calls=%fused_computation.17 | convolution fusion | flops 4854407168 | bytes 20746240 | tf_op jit(solution)/shard_map/dot_general | solution.py:168
  331.4 41.0 %all-gather.19.cloned.1.call-done = bf16[2048,1024]{0,1:T(8,128)(2,1)} async-done(((bf16[2048,64]{0,1:T(8,128)(2,1)}), bf16[2048,1024]{0,1:T(8,128)(2,1)}) %all-gather.19.cloned.1.call-update) | async-done | bytes 4194320 | tf_op jit(solution)/shard_map/all_gather | solution.py:143
  372.4 36.9 %all-gather.21.cloned.1.call-done = bf16[1154,1024]{1,0:T(8,128)(2,1)} async-done(((bf16[1154,512]{1,0:T(8,128)(2,1)}), bf16[1154,1024]{1,0:T(8,128)(2,1)}) %all-gather.21.cloned.1.call-update) | async-done | bytes 2363408 | tf_op jit(solution)/shard_map/all_gather | solution.py:28
  409.3 11.8 %fusion.47 = (f32[2048]{0:T(1024)S(1)}, bf16[1154,2048]{1,0:T(8,128)(2,1)S(1)}) fusion(f32[1154,2048]{1,0:T(8,128)} %get-tuple-element.57, bf16[1154,1024]{1,0:T(8,128)(2,1)} %all-gather.21.cloned.1.call-done, bf16[2048,1024]{0,1:T(8,128)(2,1)} %all-gather.19.cloned.1.call-done), kind=kOutput, calls=%fused_computation.103 | convolution fusion | flops 4866222080 | bytes 20746240 | tf_op jit(solution)/shard_map/dot_general | solution.py:16
  440.5 50.4 %reduce-scatter.13.cloned.1.call-done = f32[1154,512]{1,0:T(8,128)} async-done(((f32[1154,1024]{1,0:T(8,128)}), f32[1154,512]{1,0:T(8,128)}) %reduce-scatter.13.cloned.1.call-update) | async-done | bytes 2363408 | tf_op jit(solution)/shard_map/reduce_scatter | solution.py:32
  500.5 52.9 %reduce-scatter.11.cloned.1.call-done = f32[1154,512]{1,0:T(8,128)} async-done(((f32[1154,1024]{1,0:T(8,128)}), f32[1154,512]{1,0:T(8,128)}) %reduce-scatter.11.cloned.1.call-update) | async-done | bytes 2363408 | tf_op jit(solution)/shard_map/reduce_scatter | solution.py:32
  582.4 14.6 %all-gather.23.cloned.1.call-done = bf16[1154,1024]{1,0:T(8,128)(2,1)} async-done(((bf16[1154,512]{1,0:T(8,128)(2,1)}), bf16[1154,1024]{1,0:T(8,128)(2,1)}) %all-gather.23.cloned.1.call-update) | async-done | bytes 2363408 | tf_op jit(solution)/shard_map/all_gather | solution.py:28
  612.1 15.2 %multiply_convert_fusion = bf16[2,8,577,577]{2,3,1,0:T(8,128)(2,1)} fusion(f32[2,8,577,577]{2,3,1,0:T(8,128)} %get-tuple-element.55, f32[2,8,577]{2,1,0:T(8,128)S(1)} %bitcast.78, f32[2,8,577]{2,1,0:T(8,128)S(1)} %log_add_fusion, bf16[2,577,8,64]{1,3,2,0:T(8,128)(2,1)S(1)} %copy.41, bf16[2,577,8,3,64]{1,4,2,0,3:T(8,128)(2,1)} %copy-done), kind=kOutput, calls=%fused_computation | convolution fusion | flops 708472832 | bytes 37140640 | tf_op jit(solution)/shard_map/sqhd,skhd->shqk/dot_general | solution.py:92
  627.3 10.2 fusion.32
  645.6 11.3 %bitcast_reduce_fusion = (f32[8,64]{1,0:T(8,128)S(1)}, bf16[2,8,64,577]{3,2,1,0:T(8,128)(2,1)}) fusion(bf16[2,577,8,64]{1,3,2,0:T(8,128)(2,1)S(1)} %copy.41, f32[2,8,577,577]{2,3,1,0:T(8,128)} %get-tuple-element.55, f32[2,8,577]{2,1,0:T(8,128)S(1)} %log_add_fusion), kind=kOutput, calls=%fused_computation.35 | convolution fusion | flops 699000384 | bytes 23709824 | tf_op jit(solution)/shard_map/shqk,sqhd->skhd/dot_general | solution.py:104
  695.9 53.3 %reduce-scatter.23.cloned.1.call-done = bf16[2048,64]{0,1:T(8,128)(2,1)} async-done(((bf16[2048,1024]{0,1:T(8,128)(2,1)}), bf16[2048,64]{0,1:T(8,128)(2,1)}) %reduce-scatter.23.cloned.1.call-update) | async-done | bytes 262160 | tf_op jit(solution)/shard_map/reduce_scatter | solution.py:222
  751.0 59.0 %reduce-scatter.19.cloned.1.call-done = bf16[512,64]{0,1:T(8,128)(2,1)} async-done(((bf16[512,1024]{0,1:T(8,128)(2,1)}), bf16[512,64]{0,1:T(8,128)(2,1)}) %reduce-scatter.19.cloned.1.call-update) | async-done | bytes 65552 | tf_op jit(solution)/shard_map/reduce_scatter | solution.py:219
  811.5 67.6 %reduce-scatter.17.cloned.1.call-done = bf16[64,1536]{1,0:T(8,128)(2,1)} async-done(((bf16[1024,1536]{1,0:T(8,128)(2,1)}), bf16[64,1536]{1,0:T(8,128)(2,1)}) %reduce-scatter.17.cloned.1.call-update) | async-done | bytes 196624 | tf_op jit(solution)/shard_map/reduce_scatter | solution.py:211
  880.8 59.7 %reduce-scatter.15.cloned.1.call-done = f32[1154,512]{1,0:T(8,128)} async-done(((f32[1154,1024]{1,0:T(8,128)}), f32[1154,512]{1,0:T(8,128)}) %reduce-scatter.15.cloned.1.call-update) | async-done | bytes 2363408 | tf_op jit(solution)/shard_map/reduce_scatter | solution.py:32
  950.5 59.5 %all-reduce = (f32[512]{0:T(512)}, f32[512]{0:T(512)}, f32[1024]{0:T(1024)}, f32[512]{0:T(512)}, f32[512]{0:T(512)}, /*index=5*/f32[512]{0:T(512)}, f32[2048]{0:T(1024)}, f32[512]{0:T(512)}) all-reduce(f32[512]{0:T(512)S(1)} %get-tuple-element.16, f32[512]{0:T(512)S(1)} %get-tuple-element.21, ...), channel_id=1, replica_groups=mesh['wide'=16,'narrow'=2] {'wide'}, use_global_device_ids=true, to_apply=%region_24.25 | all-reduce | flops 6144 | bytes 49152 | tf_op jit(solution)/shard_map/psum | solution.py:226
  (141 shorter events, 192.4 us)
Async XLA Ops:
  7.2 51.5 %all-gather.9.cloned.1.call-start = ((), (), s32[]{:S(2)}) async-start(), calls=%async_computation.8 | async-start | bytes 3563520 | tf_op jit(solution)/shard_map/all_gather | solution.py:28
  22.0 84.4 %all-gather.11.cloned.1.call-start = ((), (), s32[]{:S(2)}) async-start(), calls=%async_computation.9 | async-start | bytes 3342336 | tf_op jit(solution)/shard_map/all_gather | solution.py:138
  22.7 143.4 %all-gather.13.cloned.1.call-start = ((), (), s32[]{:S(2)}) async-start(), calls=%async_computation.10 | async-start | bytes 1114112 | tf_op jit(solution)/shard_map/all_gather | solution.py:142
  23.5 207.2 %reduce-scatter.9.cloned.1.call-start = ((), (), s32[]{:S(2)}) async-start(), calls=%async_computation.11 | async-start | bytes 7127040 | tf_op jit(solution)/shard_map/reduce_scatter | solution.py:32
  171.7 111.4 %all-gather.17.cloned.1.call-start = ((), (), s32[]{:S(2)}) async-start(), calls=%async_computation.13 | async-start | bytes 4456448 | tf_op jit(solution)/shard_map/all_gather | solution.py:139
  172.3 147.6 %all-gather.15.cloned.1.call-start = ((), (), s32[]{:S(2)}) async-start(), calls=%async_computation.12 | async-start | bytes 3563520 | tf_op jit(solution)/shard_map/all_gather | solution.py:28
  173.0 68.6 %copy-start.14 = (f32[512]{0:T(512)S(1)}, f32[512]{0:T(512)}, u32[]{:S(2)}) copy-start(f32[512]{0:T(512)} %param.23) | copy-start | bytes 6148
  173.0 68.6 %copy-start.18 = (f32[512]{0:T(512)S(1)}, f32[512]{0:T(512)}, u32[]{:S(2)}) copy-start(f32[512]{0:T(512)} %param.24) | copy-start | bytes 6148
  241.6 78.3 %copy-start.25 = (f32[2048]{0:T(1024)S(1)}, f32[2048]{0:T(1024)}, u32[]{:S(2)}) copy-start(f32[2048]{0:T(1024)} %param.26) | copy-start | bytes 24580
  243.1 129.4 %all-gather.19.cloned.1.call-start = ((), (), s32[]{:S(2)}) async-start(), calls=%async_computation.14 | async-start | bytes 4456448 | tf_op jit(solution)/shard_map/all_gather | solution.py:143
  243.8 165.5 %all-gather.21.cloned.1.call-start = ((), (), s32[]{:S(2)}) async-start(), calls=%async_computation.16 | async-start | bytes 3563520 | tf_op jit(solution)/shard_map/all_gather | solution.py:28
  244.6 246.3 %reduce-scatter.13.cloned.1.call-start = ((), (), s32[]{:S(2)}) async-start(), calls=%async_computation.17 | async-start | bytes 7127040 | tf_op jit(solution)/shard_map/reduce_scatter | solution.py:32
  430.2 123.2 %reduce-scatter.11.cloned.1.call-start = ((), (), s32[]{:S(2)}) async-start(), calls=%async_computation.15 | async-start | bytes 7127040 | tf_op jit(solution)/shard_map/reduce_scatter | solution.py:32
  440.2 113.2 %copy-start.19 = (f32[512]{0:T(512)S(1)}, f32[512]{0:T(512)}, u32[]{:S(2)}) copy-start(f32[512]{0:T(512)} %param.28) | copy-start | bytes 6148
  440.2 156.8 %all-gather.23.cloned.1.call-start = ((), (), s32[]{:S(2)}) async-start(), calls=%async_computation.18 | async-start | bytes 3563520 | tf_op jit(solution)/shard_map/all_gather | solution.py:28
  560.5 133.5 %reduce-scatter.21.cloned.1.call-start = ((), (), s32[]{:S(2)}) async-start(), calls=%async_computation.22 | async-start | bytes 4456448 | tf_op jit(solution)/shard_map/reduce_scatter | solution.py:214
  571.0 178.1 %reduce-scatter.23.cloned.1.call-start = ((), (), s32[]{:S(2)}) async-start(), calls=%async_computation.23 | async-start | bytes 4456448 | tf_op jit(solution)/shard_map/reduce_scatter | solution.py:222
  582.3 227.7 %reduce-scatter.19.cloned.1.call-start = ((), (), s32[]{:S(2)}) async-start(), calls=%async_computation.21 | async-start | bytes 1114112 | tf_op jit(solution)/shard_map/reduce_scatter | solution.py:219
  657.0 222.2 %reduce-scatter.17.cloned.1.call-start = ((), (), s32[]{:S(2)}) async-start(), calls=%async_computation.20 | async-start | bytes 3342336 | tf_op jit(solution)/shard_map/reduce_scatter | solution.py:211
  683.7 256.8 %reduce-scatter.15.cloned.1.call-start = ((), (), s32[]{:S(2)}) async-start(), calls=%async_computation.19 | async-start | bytes 7127040 | tf_op jit(solution)/shard_map/reduce_scatter | solution.py:32
  693.9 246.7 %copy-start.2 = (bf16[1154,512]{1,0:T(8,128)(2,1)S(1)}, bf16[1154,512]{1,0:T(8,128)(2,1)}, u32[]{:S(2)}) copy-start(bf16[1154,512]{1,0:T(8,128)(2,1)} %param.15) | copy-start | bytes 3545092
  693.9 246.7 %copy-start.11 = (f32[1154]{0:T(1024)S(1)}, f32[1154]{0:T(1024)}, u32[]{:S(2)}) copy-start(f32[1154]{0:T(1024)} %copy-done.10) | copy-start | bytes 13852
  693.9 246.6 %copy-start.13 = (f32[1154]{0:T(1024)S(1)}, f32[1154]{0:T(1024)}, u32[]{:S(2)}) copy-start(f32[1154]{0:T(1024)} %copy-done.12) | copy-start | bytes 13852
  693.9 246.6 %copy-start.15 = (f32[512]{0:T(512)S(1)}, f32[512]{0:T(512)}, u32[]{:S(2)}) copy-start(f32[512]{0:T(512)} %param.17) | copy-start | bytes 6148
  (19 other events, 167.8 us)
Sparse Core Ops, SparseCore 0:
  22.1 36.4 all-gather.8
  60.9 45.4 all-gather.10
  108.6 36.1 all-gather.12
  171.8 58.7 reduce-scatter.8
  232.7 50.3 all-gather.16
  285.1 34.7 all-gather.14
  322.0 50.3 all-gather.18
  374.5 34.7 all-gather.20
  430.4 60.4 reduce-scatter.12
  493.0 60.4 reduce-scatter.10
  560.6 36.2 all-gather.22
  600.7 72.7 reduce-scatter.20
  677.3 71.7 reduce-scatter.22
  753.2 56.7 reduce-scatter.18
  813.7 65.3 reduce-scatter.16
  881.3 59.2 reduce-scatter.14
where the time goes:
time: 1030 us; the launch traced here: 1020 us
  waiting for transfers between devices  654 us (63%)
  matrix products  165 us (16%)
  blocking collectives  90.1 us (9%)
  other arithmetic  47.4 us (5%)
  local copies, waits for them, and re-layouts  46.6 us (5%)
  between operations  15.2 us (1%)
    reduce_scatter x4, waiting for transfers between devices, narrow_sum(): lax.psum_scatter(partial_rows, 'narrow', scatter_dimension=1, tiled=True)  221 us
    all_gather x4, waiting for transfers between devices, widen_rows(): return lax.all_gather(piece_rows, 'narrow', axis=1, tiled=True)  123 us
    reduce_scatter x1, waiting for transfers between devices, shards(): lax.psum_scatter(grad_w_qkv.astype(jnp.bfloat16), 'wide', scatter_dimensi...  67.6 us
    psum x1, blocking collectives, shards(): lax.psum((grad_ln1_gain, grad_ln1_bias, grad_qv_bias, jnp.sum(masked1, ax...  59.5 us
    reduce_scatter x1, waiting for transfers between devices, shards(): lax.psum_scatter(grad_w_proj.astype(jnp.bfloat16), 'wide', scatter_dimens...  59 us
    reduce_scatter x1, waiting for transfers between devices, shards(): lax.psum_scatter(grad_w_fc2.astype(jnp.bfloat16), 'wide', scatter_dimensi...  53.3 us
    all_gather x1, waiting for transfers between devices, shards(): lax.all_gather(w_qkv, 'wide', axis=0, tiled=True)  47.8 us
    all_gather x1, waiting for transfers between devices, shards(): lax.all_gather(w_fc2, 'wide', axis=1, tiled=True)  41 us
  transfers between devices with their start and end apart: 16, of which 14 were waited for; matrix products, arithmetic and copies ran while one was open for 20% of the time, Pallas kernels for 0%

commit v1 on v0

v1 whole, which is shorter than its diff:
```python
import functools
import math

import jax
import jax.numpy as jnp
from jax import lax
from jax.experimental import pallas as pl
from jax.experimental.pallas import tpu as pltpu
from jax.sharding import PartitionSpec as P

DH = 64
SEQ = 577
ROW_TILE = 16


norm_eps = 1e-06
NT = (((1,), (1,)), ((), ()))
TN = (((0,), (0,)), ((), ()))
NN = (((1,), (0,)), ((), ()))


def dot_f32(left_mat, right_mat, dims=NN):
    return lax.dot_general(left_mat, right_mat, dims, preferred_element_type=jnp.float32)


def swap(piece):
    return lax.ppermute(piece, "narrow", ((0, 1), (1, 0)))


def widen(piece, me, size):
    if size != 2:
        return lax.all_gather(piece, "narrow", axis=1, tiled=True)
    other = swap(piece)
    return jnp.concatenate(
        [jnp.where(me == 0, piece, other), jnp.where(me == 0, other, piece)], axis=1
    )


def sum_whole(partial_rows, size):
    if size != 2:
        return lax.psum(partial_rows, "narrow")
    mine = partial_rows.astype(jnp.bfloat16)
    return mine.astype(jnp.float32) + swap(mine).astype(jnp.float32)


def sum_own(left_mat, right_rows, me, size, width):
    if size != 2:
        return lax.psum_scatter(
            dot_f32(left_mat, right_rows, NT), "narrow", scatter_dimension=1, tiled=True
        )
    theirs = lax.dynamic_slice_in_dim(right_rows, (1 - me) * width, width, 0)
    ours = lax.dynamic_slice_in_dim(right_rows, me * width, width, 0)
    moved = swap(dot_f32(left_mat, theirs, NT).astype(jnp.bfloat16))
    return dot_f32(left_mat, ours, NT) + moved.astype(jnp.float32)


def normal_cdf(values_in):
    return 0.5 * (1.0 + lax.erf(values_in * (1.0 / math.sqrt(2.0))))


def gelu_exact(values_in):
    return values_in * normal_cdf(values_in)


def gelu_slope(values_in):
    return normal_cdf(values_in) + values_in * jnp.exp(-0.5 * values_in * values_in) * (
        1.0 / math.sqrt(2.0 * math.pi)
    )


def norm_forward(rows_in, gain_vec, shift_vec):
    width = float(rows_in.shape[1])
    center = jnp.sum(rows_in, axis=1, keepdims=True) / width
    spread = jnp.sum(rows_in * rows_in, axis=1, keepdims=True) / width - center * center
    inv_std = lax.rsqrt(spread + norm_eps)
    normalized = (rows_in - center) * inv_std
    return (normalized, inv_std, (normalized * gain_vec + shift_vec).astype(jnp.bfloat16))


def scores_by_key(queries, key_rows, score_scale):
    scores = dot_f32(key_rows, queries, NT) * score_scale
    key_index = lax.broadcasted_iota(jnp.int32, scores.shape, 0)
    return jnp.where(key_index < SEQ, scores, -1e30)


def attend_kernel(qkv_ref, mixed_ref, logsum_ref, *, heads, score_scale):
    for head in range(heads):
        base = head * 3 * DH
        queries = qkv_ref[:, base : base + DH]
        key_rows = qkv_ref[:, base + DH : base + 2 * DH]
        value_rows = qkv_ref[:, base + 2 * DH : base + 3 * DH]
        scores = scores_by_key(queries, key_rows, score_scale)
        top = jnp.max(scores, axis=0, keepdims=True)
        exp_scores = jnp.exp(scores - top)
        total = jnp.sum(exp_scores, axis=0, keepdims=True)
        probs = (exp_scores * (1.0 / total)).astype(jnp.bfloat16)
        mixed_ref[:, head * DH : (head + 1) * DH] = dot_f32(probs, value_rows, TN).astype(
            jnp.bfloat16
        )
        logsum_ref[0, head : head + 1, :] = top + jnp.log(total)


def attend_back_kernel(
    qkv_ref, mixed_ref, d_mixed_ref, logsum_ref, d_qkv_ref, sums_ref, *, heads, score_scale
):
    for head in range(heads):
        base = head * 3 * DH
        queries = qkv_ref[:, base : base + DH]
        key_rows = qkv_ref[:, base + DH : base + 2 * DH]
        value_rows = qkv_ref[:, base + 2 * DH : base + 3 * DH]
        mixed = mixed_ref[:, head * DH : (head + 1) * DH]
        d_mixed = d_mixed_ref[:, head * DH : (head + 1) * DH]
        products = d_mixed.astype(jnp.float32) * mixed.astype(jnp.float32)
        delta = jnp.sum(jnp.transpose(products), axis=0, keepdims=True)
        scores = scores_by_key(queries, key_rows, score_scale)
        probs = jnp.exp(scores - logsum_ref[0, head : head + 1, :])
        d_probs = dot_f32(value_rows, d_mixed, NT)
        d_scores = (probs * (d_probs - delta)).astype(jnp.bfloat16)
        d_query = dot_f32(d_scores, key_rows, TN) * score_scale
        d_keys = dot_f32(d_scores, queries, NN) * score_scale
        d_values = dot_f32(probs.astype(jnp.bfloat16), d_mixed, NN)
        for part, grad in enumerate((d_query, d_keys, d_values)):
            columns = slice(base + part * DH, base + (part + 1) * DH)
            d_qkv_ref[:, columns] = grad.astype(jnp.bfloat16)
            sums_ref[0, :, columns] = jnp.broadcast_to(
                jnp.sum(grad, axis=0, keepdims=True), (8, DH)
            )


def head_pairs(width):
    heads = 2
    return heads, width // (3 * DH * heads)


def attend(qkv_rows, slot_rows, score_scale):
    row_count, width = qkv_rows.shape
    slots = row_count // slot_rows
    heads, pairs = head_pairs(width)
    return pl.pallas_call(
        functools.partial(attend_kernel, heads=heads, score_scale=score_scale),
        grid=(slots, pairs),
        in_specs=[pl.BlockSpec((slot_rows, heads * 3 * DH), lambda s, p: (s, p))],
        out_specs=[
            pl.BlockSpec((slot_rows, heads * DH), lambda s, p: (s, p)),
            pl.BlockSpec((1, 8, slot_rows), lambda s, p: (s * pairs + p, 0, 0)),
        ],
        out_shape=[
            jax.ShapeDtypeStruct((row_count, width // 3), jnp.bfloat16),
            jax.ShapeDtypeStruct((slots * pairs, 8, slot_rows), jnp.float32),
        ],
        cost_estimate=pl.CostEstimate(
            flops=4 * slots * pairs * heads * slot_rows * slot_rows * 256,
            bytes_accessed=row_count * width * 3,
            transcendentals=slots * pairs * heads * slot_rows * slot_rows,
        ),
        name="attend",
    )(qkv_rows)


def attend_backward(qkv_rows, mixed_rows, d_mixed, logsum, slot_rows, score_scale):
    row_count, width = qkv_rows.shape
    slots = row_count // slot_rows
    heads, pairs = head_pairs(width)
    narrow_block = pl.BlockSpec((slot_rows, heads * DH), lambda s, p: (s, p))
    wide_block = pl.BlockSpec((slot_rows, heads * 3 * DH), lambda s, p: (s, p))
    return pl.pallas_call(
        functools.partial(attend_back_kernel, heads=heads, score_scale=score_scale),
        grid=(slots, pairs),
        in_specs=[
            wide_block,
            narrow_block,
            narrow_block,
            pl.BlockSpec((1, 8, slot_rows), lambda s, p: (s * pairs + p, 0, 0)),
        ],
        out_specs=[
            wide_block,
            pl.BlockSpec((1, 8, heads * 3 * DH), lambda s, p: (s, 0, p)),
        ],
        out_shape=[
            jax.ShapeDtypeStruct((row_count, width), jnp.bfloat16),
            jax.ShapeDtypeStruct((slots, 8, width), jnp.float32),
        ],
        cost_estimate=pl.CostEstimate(
            flops=10 * slots * pairs * heads * slot_rows * slot_rows * 256,
            bytes_accessed=row_count * width * 6,
            transcendentals=slots * pairs * heads * slot_rows * slot_rows,
        ),
        name="attend_back",
    )(qkv_rows, mixed_rows, d_mixed, logsum)


def shards(
    inputs,
    counts,
    ln1_gain,
    ln1_bias,
    w_qkv,
    qv_bias,
    w_proj,
    proj_bias,
    ln2_gain,
    ln2_bias,
    w_fc1,
    fc1_bias,
    w_fc2,
    fc2_bias,
    cotangent,
):
    size = lax.axis_size("narrow")
    me = lax.axis_index("narrow")
    row_count, width = inputs.shape
    slot_count = row_count // SEQ
    slot_rows = -(-SEQ // ROW_TILE) * ROW_TILE
    padded = slot_count * slot_rows
    head_count = w_qkv.shape[1] // (3 * DH)
    score_scale = 1.0 / math.sqrt(DH)

    def pad_rows(rows):
        rows = rows.reshape(slot_count, SEQ, rows.shape[1])
        rows = jnp.pad(rows, ((0, 0), (0, slot_rows - SEQ), (0, 0)))
        return rows.reshape(padded, rows.shape[2])

    def trim_rows(rows):
        rows = rows.reshape(slot_count, slot_rows, rows.shape[1])[:, :SEQ]
        return rows.reshape(row_count, rows.shape[2])

    def own(rows):
        return lax.dynamic_slice_in_dim(rows, me * width, width, rows.ndim - 1)

    padded_index = lax.broadcasted_iota(jnp.int32, (padded, 1), 0)
    live_rows = (
        (padded_index // slot_rows < counts[0]) & (padded_index % slot_rows < SEQ)
    ).astype(jnp.float32)

    early = lax.all_gather(
        jnp.concatenate([w_qkv, w_proj.T], axis=1), "wide", axis=0, tiled=True
    )
    wqkv_full = early[:, : w_qkv.shape[1]]
    wproj_t = early[:, w_qkv.shape[1] :]
    late = lax.all_gather(
        jnp.concatenate([w_fc1, w_fc2.T], axis=1), "wide", axis=0, tiled=True
    )
    wfc1_full = late[:, : w_fc1.shape[1]]
    wfc2_t = late[:, w_fc1.shape[1] :]

    vectors = widen(
        jnp.stack([ln1_gain, ln1_bias, ln2_gain, ln2_bias, proj_bias]), me, size
    )
    gain_one, shift_one, gain_two, shift_two, proj_shift = (vectors[i : i + 1] for i in range(5))

    inputs_whole = widen(pad_rows(inputs), me, size)
    sent2 = widen((live_rows * pad_rows(cotangent).astype(jnp.float32)).astype(jnp.bfloat16), me, size)

    resid = inputs_whole.astype(jnp.float32)
    hat_one, inv_one, normed1 = norm_forward(resid, gain_one, shift_one)
    bias_qv = qv_bias.reshape(head_count, 2, DH)
    bias_full = jnp.stack(
        [bias_qv[:, 0], jnp.zeros_like(bias_qv[:, 0]), bias_qv[:, 1]], axis=1
    ).reshape(1, head_count * 3 * DH)
    qkv_rows = (dot_f32(normed1, wqkv_full) + bias_full).astype(jnp.bfloat16)
    qkv_rows, sent2 = lax.optimization_barrier((qkv_rows, sent2))
    mixed_rows, logsum = attend(qkv_rows, slot_rows, score_scale)
    attn_out = sum_whole(dot_f32(mixed_rows, wproj_t, NT), size) + proj_shift
    resid_mid = resid + live_rows * attn_out
    hat_two, inv_two, normed2 = norm_forward(resid_mid, gain_two, shift_two)
    inner_pre = dot_f32(normed2, wfc1_full) + fc1_bias
    activation = gelu_exact(inner_pre).astype(jnp.bfloat16)

    d_inner = dot_f32(sent2, wfc2_t) * gelu_slope(inner_pre)
    d_inner_b = d_inner.astype(jnp.bfloat16)
    d_norm2 = sum_whole(dot_f32(d_inner_b, wfc1_full, NT), size)
    grad_fc = jnp.concatenate(
        [
            dot_f32(normed2, d_inner_b, TN).astype(jnp.bfloat16),
            dot_f32(sent2, activation, TN).astype(jnp.bfloat16),
        ],
        axis=1,
    )
    d_norm2, _ = lax.optimization_barrier((d_norm2, grad_fc))
    grad_fc = lax.psum_scatter(grad_fc, "wide", scatter_dimension=0, tiled=True)

    mlp_out = sum_own(activation, wfc2_t, me, size, width) + fc2_bias
    output = trim_rows((own(resid_mid) + live_rows * mlp_out).astype(jnp.bfloat16))

    full_width = float(width * size)
    scaled = d_norm2 * gain_two
    back_two = inv_two * (
        scaled
        - jnp.sum(scaled, axis=1, keepdims=True) / full_width
        - hat_two * (jnp.sum(scaled * hat_two, axis=1, keepdims=True) / full_width)
    )
    own_norm2 = own(d_norm2)
    grad_ln2_gain = jnp.sum(own_norm2 * own(hat_two), axis=0)
    grad_ln2_bias = jnp.sum(own_norm2, axis=0)
    own_cot = pad_rows(cotangent).astype(jnp.float32)
    masked1 = live_rows * (sent2.astype(jnp.float32) + back_two)
    own_mid = own_cot + own(back_two)
    sent1 = masked1.astype(jnp.bfloat16)
    d_mixed = dot_f32(sent1, wproj_t).astype(jnp.bfloat16)
    d_qkv_b, qkv_sums = attend_backward(
        qkv_rows, mixed_rows, d_mixed, logsum, slot_rows, score_scale
    )
    grad_attn = jnp.concatenate(
        [
            dot_f32(normed1, d_qkv_b, TN).astype(jnp.bfloat16),
            dot_f32(sent1, mixed_rows, TN).astype(jnp.bfloat16),
        ],
        axis=1,
    )
    grad_attn = lax.psum_scatter(grad_attn, "wide", scatter_dimension=0, tiled=True)
    qkv_sums = jnp.sum(qkv_sums[:, 0], axis=0).reshape(head_count, 3, DH)
    grad_qv_bias = jnp.stack([qkv_sums[:, 0], qkv_sums[:, 2]], axis=1).reshape(-1)

    part1 = dot_f32(d_qkv_b, wqkv_full, NT)
    scaled_part = part1 * gain_one
    row_sums = jnp.stack([jnp.sum(scaled_part, axis=1), jnp.sum(scaled_part * hat_one, axis=1)])
    if size == 2:
        row_sums = row_sums + swap(row_sums)
        moved = swap(
            lax.dynamic_slice_in_dim(part1, (1 - me) * width, width, 1).astype(jnp.bfloat16)
        )
        d_norm1 = own(part1) + moved.astype(jnp.float32)
    else:
        row_sums = lax.psum(row_sums, "narrow")
        d_norm1 = lax.psum_scatter(part1, "narrow", scatter_dimension=1, tiled=True)
    own_hat = own(hat_one)
    back_one = inv_one * (
        d_norm1 * ln1_gain
        - row_sums[0][:, None] / full_width
        - own_hat * (row_sums[1][:, None] / full_width)
    )
    grad_in = trim_rows((own_mid + back_one).astype(jnp.bfloat16))

    vectors_out = [
        jnp.sum(d_norm1 * own_hat, axis=0),
        jnp.sum(d_norm1, axis=0),
        grad_qv_bias,
        jnp.sum(own(masked1), axis=0),
        grad_ln2_gain,
        grad_ln2_bias,
        jnp.sum(d_inner, axis=0),
        jnp.sum(live_rows * own_cot, axis=0),
    ]
    joined = jnp.concatenate(vectors_out)
    joined = lax.psum(joined.reshape(-1, 128), "wide").reshape(-1)
    summed, at = [], 0
    for vector in vectors_out:
        summed.append(joined[at : at + vector.shape[0]])
        at += vector.shape[0]
    qkv_columns, fc_columns = w_qkv.shape[1], w_fc1.shape[1]
    grad_w_qkv = grad_attn[:, :qkv_columns].astype(jnp.float32)
    grad_w_proj = grad_attn[:, qkv_columns:].T.astype(jnp.float32)
    grad_w_fc1 = grad_fc[:, :fc_columns].astype(jnp.float32)
    grad_w_fc2 = grad_fc[:, fc_columns:].T.astype(jnp.float32)
    return (
        output,
        grad_in,
        summed[0],
        summed[1],
        grad_w_qkv,
        summed[2],
        grad_w_proj,
        summed[3],
        summed[4],
        summed[5],
        grad_w_fc1,
        summed[6],
        grad_w_fc2,
        summed[7],
    )


def solution(mesh):
    return jax.shard_map(
        shards,
        mesh=mesh,
        in_specs=(
            P("wide", "narrow"),
            P("wide"),
            P("narrow"),
            P("narrow"),
            P("wide", "narrow"),
            P("narrow"),
            P("narrow", "wide"),
            P("narrow"),
            P("narrow"),
            P("narrow"),
            P("wide", "narrow"),
            P("narrow"),
            P("narrow", "wide"),
            P("narrow"),
            P("wide", "narrow"),
        ),
        out_specs=(
            P("wide", "narrow"),
            P("wide", "narrow"),
            P("narrow"),
            P("narrow"),
            P("wide", "narrow"),
            P("narrow"),
            P("narrow", "wide"),
            P("narrow"),
            P("narrow"),
            P("narrow"),
            P("wide", "narrow"),
            P("narrow"),
            P("narrow", "wide"),
            P("narrow"),
        ),
        check_vma=False,
    )
```

time: 1030 us -> 499 us (0.48)
  waiting for transfers between devices: 654 us -> 192 us
  matrix products: 165 us -> 95 us
  Pallas kernels: 0 us -> 46 us
  blocking collectives: 90.1 us -> 60.5 us
  local copies, waits for them, and re-layouts: 46.6 us -> 22.3 us
    reduce_scatter x8 -> x2, waiting for transfers between devices: 401 us -> 22.5 us  [the longest x1 22.5 us: shards(): grad_fc = lax.psum_scatter(grad_fc, 'wide', scatter_dimension=0, tiled=True)]
    all_gather x8 -> x2, waiting for transfers between devices: 250 us -> 0.01 us  [the longest x1 0.01 us: shards(): lax.all_gather(jnp.concatenate([w_qkv, w_proj.T], axis=1), 'wide', axis=0...]
    ppermute x0 -> x8, waiting for transfers between devices: none -> 169 us  [swap(): return lax.ppermute(piece, 'narrow', ((0, 1), (1, 0)))]
    dot_general x18 -> x13, matrix products: 165 us -> 95 us  [dot_f32(): lax.dot_general(left_mat, right_mat, dims, preferred_element_type=jnp.flo...]
    pallas_call x0 -> x2, Pallas kernels: none -> 46 us  [the longest x1 27.4 us: attend_backward(): pl.pallas_call(functools.partial(attend_back_kernel, heads=heads, score_s...]
    psum x5 -> x1, blocking collectives: 90.1 us -> 60.5 us  [shards(): joined = lax.psum(joined.reshape(-1, 128), 'wide').reshape(-1)]
    concatenate x0 -> x5, other arithmetic: none -> 15.8 us  [the longest x1 7.8 us: shards(): jnp.concatenate([dot_f32(normed2, d_inner_b, TN).astype(jnp.bfloat16), do...]
    convert_element_type x10 -> x6, other arithmetic: 19.8 us -> 6.71 us  [the longest x1 2.1 us: shards(): grad_w_fc2 = grad_fc[:, fc_columns:].T.astype(jnp.float32)]
  transfers between devices with their start and end apart: 16 -> 12, of which waited for: 14 -> 7; matrix products, arithmetic and copies ran while one was open for 20% -> 21% of each run, Pallas kernels for 0% -> 4%
where the time goes in v1:
time: 499 us; the launch traced here: 493 us
  waiting for transfers between devices  192 us (38%)
  matrix products  95 us (19%)
  blocking collectives  60.5 us (12%)
  other arithmetic  51.9 us (10%)
  Pallas kernels  46 us (9%)
  local copies, waits for them, and re-layouts  22.3 us (4%)
  between operations  15.3 us (3%)
  starting transfers between devices  10.2 us (2%)
    ppermute x8, waiting for transfers between devices, swap(): return lax.ppermute(piece, 'narrow', ((0, 1), (1, 0)))  169 us
    dot_general x13, matrix products, dot_f32(): lax.dot_general(left_mat, right_mat, dims, preferred_element_type=jnp.flo...  95 us
    psum x1, blocking collectives, shards(): joined = lax.psum(joined.reshape(-1, 128), 'wide').reshape(-1)  60.5 us
    pallas_call x1, Pallas kernels, attend_backward(): pl.pallas_call(functools.partial(attend_back_kernel, heads=heads, score_s...  27.4 us
    reduce_scatter x1, waiting for transfers between devices, shards(): grad_fc = lax.psum_scatter(grad_fc, 'wide', scatter_dimension=0, tiled=True)  22.5 us
    pallas_call x1, Pallas kernels, attend(): pl.pallas_call(functools.partial(attend_kernel, heads=heads, score_scale=...  18.6 us
  transfers between devices with their start and end apart: 12, of which 7 were waited for; matrix products, arithmetic and copies ran while one was open for 21% of the time, Pallas kernels for 4%

profile of v1, /device:TPU:0, one launch (start us, length us, event | category | flops | bytes accessed | tf_op | source)
XLA Modules:
  0.0 493.3 jit_solution(6636255754462201777)
XLA Ops:
  22.4 23.7 %collective-permute-done = bf16[1184,512]{1,0:T(8,128)(2,1)} collective-permute-done((bf16[1184,512]{1,0:T(8,128)(2,1)S(1)}, bf16[1184,512]{1,0:T(8,128)(2,1)}, u32[]{:S(2)}, u32[]{:S(2)}) %collective-permute-start) | collective-permute-done | bytes 1212448 | tf_op jit(solution)/shard_map/ppermute | solution.py:27
  49.8 20.9 %collective-permute-done.2 = bf16[1184,512]{1,0:T(8,128)(2,1)} collective-permute-done((bf16[1184,512]{1,0:T(8,128)(2,1)}, bf16[1184,512]{1,0:T(8,128)(2,1)}, u32[]{:S(2)}, u32[]{:S(2)}) %collective-permute-start.2) | collective-permute-done | bytes 1212448 | tf_op jit(solution)/shard_map/ppermute | solution.py:27
  74.3 8.3 %fusion.5.qkv_ref = bf16[1184,1536]{1,0:T(8,128)(2,1)} fusion(f32[1536]{0:T(1024)S(1)} %add.162, bf16[1024,2048]{1,0:T(8,128)(2,1)} %all-gather.3.cloned.1.call-done, f32[1024]{0:T(1024)S(1)} %bitcast.85, f32[1024]{0:T(1024)S(1)} %bitcast.82, f32[1184]{0:T(1024)S(1)} %get-tuple-element.71, f32[1184]{0:T(1024)S(1)} %get-tuple-element.70, ...), kind=kOutput, calls=%fused_computation.15 | convolution fusion | flops 3739090944 | bytes 9231616 | tf_op jit(solution)/shard_map/dot_general | solution.py:23
  82.6 18.6 %attend.1 = (bf16[1184,512]{1,0:T(8,128)(2,1)}, f32[8,8,592]{2,1,0:T(8,128)}) custom-call(bf16[1184,1536]{1,0:T(8,128)(2,1)} %fusion.5.qkv_ref), custom_call_target="tpu_custom_call" | custom-call | flops 5742002176 | bytes 5455872 | tf_op jit(solution)/shard_map/attend/pallas_call | solution.py:139
  105.0 53.0 %collective-permute-done.3 = bf16[1184,1024]{1,0:T(8,128)(2,1)S(1)} collective-permute-done((bf16[1184,1024]{1,0:T(8,128)(2,1)S(1)}, bf16[1184,1024]{1,0:T(8,128)(2,1)S(1)}, u32[]{:S(2)}, u32[]{:S(2)}) %collective-permute-start.3) | collective-permute-done | bytes 2424864 | tf_op jit(solution)/shard_map/ppermute | solution.py:27
  165.6 11.9 %multiply_convert_fusion = (bf16[1184,2048]{1,0:T(8,128)(2,1)S(1)}, f32[1184,2048]{1,0:T(8,128)}) fusion(f32[2048]{0:T(1024)S(1)} %copy-done.14, bf16[1024,4096]{1,0:T(8,128)(2,1)} %all-gather.5.cloned.1.call-done, f32[1184,1024]{1,0:T(8,128)} %subtract_multiply_fusion.1, f32[1024]{0:T(1024)S(1)} %bitcast.87, f32[1024]{0:T(1024)S(1)} %bitcast.75), kind=kOutput, calls=%fused_computation.6 | convolution fusion | flops 4984242176 | bytes 23609344 | tf_op jit(solution)/shard_map/dot_general | solution.py:23
  177.4 12.2 %fusion.51 = (f32[2048]{0:T(1024)S(1)}, bf16[1184,2048]{1,0:T(8,128)(2,1)S(1)}) fusion(f32[1184,2048]{1,0:T(8,128)} %get-tuple-element.75, bf16[1184,1024]{1,0:T(8,128)(2,1)S(1)} %copy-done.5, bf16[1024,4096]{1,0:T(8,128)(2,1)S(1)} %copy-done.10), kind=kOutput, calls=%fused_computation.141 | convolution fusion | flops 4992727040 | bytes 21176320 | tf_op jit(solution)/shard_map/dot_general | solution.py:23
  189.6 6.6 %convolution_convert_fusion.3 = bf16[1184,1024]{1,0:T(8,128)(2,1)} fusion(bf16[1024,4096]{1,0:T(8,128)(2,1)S(1)} %copy-done.10, bf16[1184,2048]{1,0:T(8,128)(2,1)S(1)} %get-tuple-element.78), kind=kOutput, calls=%fused_computation.33 | convolution fusion | flops 4967268352 | bytes 11468800 | tf_op jit(solution)/shard_map/dot_general | solution.py:23
  197.0 7.4 %convolution_convert_fusion.1 = bf16[1024,2048]{1,0:T(8,128)(2,1)} fusion(bf16[1184,1024]{1,0:T(8,128)(2,1)S(1)} %copy-done.5, bf16[1184,2048]{1,0:T(8,128)(2,1)S(1)} %get-tuple-element.74), kind=kOutput, calls=%fused_computation.31 | convolution fusion | flops 4968153088 | bytes 11468800 | tf_op jit(solution)/shard_map/dot_general | solution.py:23
  204.5 7.2 %convolution_convert_fusion.2 = bf16[1024,2048]{1,0:T(8,128)(2,1)} fusion(bf16[1184,2048]{1,0:T(8,128)(2,1)S(1)} %get-tuple-element.78, f32[1184,1024]{1,0:T(8,128)S(1)} %bitcast.69, f32[1024]{0:T(1024)S(1)} %bitcast.88, f32[1024]{0:T(1024)S(1)} %bitcast.76), kind=kOutput, calls=%fused_computation.32 | convolution fusion | flops 4971790336 | bytes 13901824 | tf_op jit(solution)/shard_map/dot_general | solution.py:23
  211.7 7.8 %pad_maximum_fusion = bf16[1024,4096]{1,0:T(8,128)(2,1)} fusion(bf16[1024,2048]{1,0:T(8,128)(2,1)} %convolution_convert_fusion.1, bf16[1024,2048]{1,0:T(8,128)(2,1)} %convolution_convert_fusion.2), kind=kLoop, calls=%fused_computation.14 | loop fusion | flops 16777216 | bytes 16777216 | tf_op jit(solution)/shard_map/concatenate | solution.py:272
  219.5 29.6 %collective-permute-done.5 = bf16[1184,1024]{1,0:T(8,128)(2,1)} collective-permute-done((bf16[1184,1024]{1,0:T(8,128)(2,1)}, bf16[1184,1024]{1,0:T(8,128)(2,1)}, u32[]{:S(2)}, u32[]{:S(2)}) %collective-permute-start.5) | collective-permute-done | bytes 2424864 | tf_op jit(solution)/shard_map/ppermute | solution.py:27
  256.1 3.9 add_multiply_fusion.1
  262.6 3.8 convolution_convert_fusion.5.d_mixed_ref
  266.4 27.4 %attend_back.1 = (bf16[1184,1536]{1,0:T(8,128)(2,1)}, f32[2,8,1536]{2,1,0:T(8,128)}) custom-call(bf16[1184,1536]{1,0:T(8,128)(2,1)} %fusion.5.qkv_ref, bf16[1184,512]{1,0:T(8,128)(2,1)} %get-tuple-element.22.mixed_ref, bf16[1184,512]{1,0:T(8,128)(2,1)} %convolution_convert_fusion.5.d_mixed_ref, f32[8,8,592]{2,1,0:T(8,128)} %get-tuple-element.25.logsum_ref), custom_call_target="tpu_custom_call" | custom-call | flops 14355005440 | bytes 10911744 | tf_op jit(solution)/shard_map/attend_back/pallas_call | solution.py:166
  293.8 7.1 %convolution_convert_fusion.4 = bf16[1024,1536]{1,0:T(8,128)(2,1)S(1)} fusion(bf16[1184,1536]{1,0:T(8,128)(2,1)} %get-tuple-element.26, f32[1024]{0:T(1024)S(1)} %bitcast.86, f32[1024]{0:T(1024)S(1)} %bitcast.83, f32[1184]{0:T(1024)S(1)} %get-tuple-element.71, f32[1184]{0:T(1024)S(1)} %get-tuple-element.70, bf16[1184,512]{1,0:T(8,128)(2,1)} %copy-done.2, ...), kind=kOutput, calls=%fused_computation.34 | convolution fusion | flops 3737026560 | bytes 9225472 | tf_op jit(solution)/shard_map/dot_general | solution.py:23
  306.8 7.7 %convolution_convert_fusion.6 = bf16[1184,512]{1,0:T(8,128)(2,1)} fusion(bf16[1184,2048]{1,0:T(8,128)(2,1)} %copy-done.17, bf16[1024,2048]{1,0:T(8,128)(2,1)S(1)} %slice.157, s32[]{:T(128)S(6)} %select_n.85), kind=kOutput, calls=%fused_computation.38 | convolution fusion | flops 2483634176 | bytes 8159236 | tf_op jit(solution)/shard_map/dot_general | solution.py:23
  316.1 24.5 %collective-permute-done.4 = bf16[1184,512]{1,0:T(8,128)(2,1)} collective-permute-done((bf16[1184,512]{1,0:T(8,128)(2,1)}, bf16[1184,512]{1,0:T(8,128)(2,1)}, u32[]{:S(2)}, u32[]{:S(2)}) %collective-permute-start.4) | collective-permute-done | bytes 1212448 | tf_op jit(solution)/shard_map/ppermute | solution.py:27
  340.5 7.0 %add_convert_fusion.2 = bf16[1184,512]{1,0:T(8,128)(2,1)S(1)} fusion(bf16[1184,512]{1,0:T(8,128)(2,1)} %collective-permute-done.4, f32[1184,1024]{1,0:T(8,128)} %copy-done, s32[]{:T(128)S(6)} %select_n.84, bf16[1184,2048]{1,0:T(8,128)(2,1)} %copy-done.17, bf16[1024,2048]{1,0:T(8,128)(2,1)} %copy-done.8, f32[512]{0:T(512)S(1)} %copy-done.15, ...), kind=kOutput, calls=%fused_computation.58 | convolution fusion | flops 2486665216 | bytes 11804288 | tf_op jit(solution)/shard_map/dot_general | solution.py:23
  351.2 10.0 %multiply_reduce_fusion.3 = (f32[1184]{0:T(1024)S(1)}, f32[1184]{0:T(1024)S(1)}, f32[1184,1024]{1,0:T(8,128)}, f32[1184,1024]{1,0:T(8,128)S(1)}) fusion(f32[1024]{0:T(1024)S(1)} %bitcast.84, f32[1184]{0:T(1024)S(1)} %get-tuple-element.71, f32[1184]{0:T(1024)S(1)} %get-tuple-element.70, bf16[1184,512]{1,0:T(8,128)(2,1)} %copy-done.2, ...), kind=kOutput, calls=%fused_computation.27 | convolution fusion | flops 3736663552 | bytes 18930176 | tf_op jit(solution)/shard_map/dot_general | solution.py:23
  372.7 17.5 %collective-permute-done.7 = f32[2,1184]{1,0:T(2,128)S(1)} collective-permute-done((f32[2,1184]{1,0:T(2,128)S(1)}, f32[2,1184]{1,0:T(2,128)S(1)}, u32[]{:S(2)}, u32[]{:S(2)}) %collective-permute-start.7) | collective-permute-done | bytes 9504 | tf_op jit(solution)/shard_map/ppermute | solution.py:27
  390.3 4.5 fusion.28
  396.2 60.5 %psum.7 = f32[48,128]{1,0:T(8,128)S(1)} all-reduce(f32[48,128]{1,0:T(8,128)S(1)} %bitcast.79), channel_id=1, replica_groups=mesh['wide'=16,'narrow'=2] {'wide'}, use_global_device_ids=true, to_apply=%region_16.17 | all-reduce | flops 6144 | bytes 49152 | tf_op jit(solution)/shard_map/psum | solution.py:345
  461.7 22.5 %reduce-scatter.5.cloned.1.call-done = bf16[64,4096]{1,0:T(8,128)(2,1)} async-done(((bf16[1024,4096]{1,0:T(8,128)(2,1)}), bf16[64,4096]{1,0:T(8,128)(2,1)}) %reduce-scatter.5.cloned.1.call-update) | async-done | bytes 524304 | tf_op jit(solution)/shard_map/reduce_scatter | solution.py:280
  (131 shorter events, 74.3 us)
Async XLA Ops:
  7.2 67.1 %all-gather.3.cloned.1.call-start = ((), (), s32[]{:S(2)}) async-start(), calls=%async_computation.2 | async-start | bytes 4456448 | tf_op jit(solution)/shard_map/all_gather | solution.py:235
  8.9 156.6 %all-gather.5.cloned.1.call-start = ((), (), s32[]{:S(2)}) async-start(), calls=%async_computation.3 | async-start | bytes 8912896 | tf_op jit(solution)/shard_map/all_gather | solution.py:240
  10.9 447.7 %reduce-scatter.3.cloned.1.call-start = ((), (), s32[]{:S(2)}) async-start(), calls=%async_computation.4 | async-start | bytes 4456448 | tf_op jit(solution)/shard_map/reduce_scatter | solution.py:310
  11.7 10.6 %collective-permute-start.1 = (f32[5,512]{1,0:T(8,128)S(1)}, f32[5,512]{1,0:T(8,128)S(1)}, u32[]{:S(2)}, u32[]{:S(2)}) collective-permute-start(f32[5,512]{1,0:T(8,128)S(1)} %stack.38), channel_id=1, source_target_pairs={{0,1},{1,0},{2,3},{3,2},{4,5},{5,4},{6,7},{7,6},{8,9},{9,8},{10,11... | collective-permute-start | bytes 30728 | tf_op jit(solution)/shard_map/ppermute | solution.py:27
  16.3 29.7 %collective-permute-start = (bf16[1184,512]{1,0:T(8,128)(2,1)S(1)}, bf16[1184,512]{1,0:T(8,128)(2,1)}, u32[]{:S(2)}, u32[]{:S(2)}) collective-permute-start(bf16[1184,512]{1,0:T(8,128)(2,1)S(1)} %bitcast.70), channel_id=1, source_target_pairs={{0,1},{1,0},{2,3},{3,2},{4,5},{5,4},{6,7},{7,6},{8,9},{9,8},{10,11... | collective-permute-start | bytes 3637256 | tf_op jit(solution)/shard_map/ppermute | solution.py:27
  20.0 50.6 %collective-permute-start.2 = (bf16[1184,512]{1,0:T(8,128)(2,1)}, bf16[1184,512]{1,0:T(8,128)(2,1)}, u32[]{:S(2)}, u32[]{:S(2)}) collective-permute-start(bf16[1184,512]{1,0:T(8,128)(2,1)} %fusion.14), channel_id=1, source_target_pairs={{0,1},{1,0},{2,3},{3,2},{4,5},{5,4},{6,7},{7,6},{8,9},{9,8},{10,11... | collective-permute-start | bytes 3637256 | tf_op jit(solution)/shard_map/ppermute | solution.py:27
  101.2 56.7 %copy-start.3 = (bf16[1184,512]{1,0:T(8,128)(2,1)S(1)}, bf16[1184,512]{1,0:T(8,128)(2,1)}, u32[]{:S(2)}) copy-start(bf16[1184,512]{1,0:T(8,128)(2,1)} %copy-done.2) | copy-start | bytes 3637252
  104.4 53.6 %collective-permute-start.3 = (bf16[1184,1024]{1,0:T(8,128)(2,1)S(1)}, bf16[1184,1024]{1,0:T(8,128)(2,1)S(1)}, u32[]{:S(2)}, u32[]{:S(2)}) collective-permute-start(bf16[1184,1024]{1,0:T(8,128)(2,1)S(1)} %convolution_convert_fusion), channel_id=1, source_target_pairs={{0,1},{1,0},{2,3},{3,2},{4,5},{5,4},{6,7},{7,6},{8,9},{9,8},{10,11... | collective-permute-start | bytes 7274504 | tf_op jit(solution)/shard_map/ppermute | solution.py:27
  165.5 11.9 %copy-start.5 = (bf16[1184,1024]{1,0:T(8,128)(2,1)S(1)}, bf16[1184,1024]{1,0:T(8,128)(2,1)}, u32[]{:S(2)}) copy-start(bf16[1184,1024]{1,0:T(8,128)(2,1)} %pad_maximum_fusion.3) | copy-start | bytes 7274500
  165.5 11.9 %copy-start.10 = (bf16[1024,4096]{1,0:T(8,128)(2,1)S(1)}, bf16[1024,4096]{1,0:T(8,128)(2,1)}, u32[]{:S(2)}) copy-start(bf16[1024,4096]{1,0:T(8,128)(2,1)} %all-gather.5.cloned.1.call-done) | copy-start | bytes 25165828
  177.4 19.6 %copy-start.17 = (bf16[1184,2048]{1,0:T(8,128)(2,1)}, bf16[1184,2048]{1,0:T(8,128)(2,1)S(1)}, u32[]{:S(2)}) copy-start(bf16[1184,2048]{1,0:T(8,128)(2,1)S(1)} %get-tuple-element.74) | copy-start | bytes 14548996
  177.4 27.0 %slice-start.2 = ((s8[4849664]{0:T(1024)(128)(4,1)}), s8[655360]{0:T(1024)(128)(4,1)S(1)}, s32[]{:S(2)}) async-start(s8[4849664]{0:T(1024)(128)(4,1)} %bitcast.68), calls=%async_computation.8 | async-start | bytes 1310720
  189.6 14.8 %slice-start.3 = ((s8[4849664]{0:T(1024)(128)(4,1)}), s8[4194304]{0:T(1024)(128)(4,1)S(1)}, s32[]{:S(2)}) async-start(s8[4849664]{0:T(1024)(128)(4,1)} %bitcast.68), calls=%async_computation.9 | async-start | bytes 8388608
  196.2 53.0 %collective-permute-start.5 = (bf16[1184,1024]{1,0:T(8,128)(2,1)}, bf16[1184,1024]{1,0:T(8,128)(2,1)}, u32[]{:S(2)}, u32[]{:S(2)}) collective-permute-start(bf16[1184,1024]{1,0:T(8,128)(2,1)} %convolution_convert_fusion.3), channel_id=1, source_target_pairs={{0,1},{1,0},{2,3},{3,2},{4,5},{5,4},{6,7},{7,6},{8,9},{9,8},{10,11... | collective-permute-start | bytes 7274504 | tf_op jit(solution)/shard_map/ppermute | solution.py:27
  219.5 33.1 %slice-start = ((s8[4849664]{0:T(1024)(128)(4,1)}), s8[655360]{0:T(1024)(128)(4,1)S(1)}, s32[]{:S(2)}) async-start(s8[4849664]{0:T(1024)(128)(4,1)} %bitcast.66), calls=%async_computation.6 | async-start | bytes 1310720
  219.5 33.2 %slice-start.1 = ((s8[4849664]{0:T(1024)(128)(4,1)}), s8[4194304]{0:T(1024)(128)(4,1)S(1)}, s32[]{:S(2)}) async-start(s8[4849664]{0:T(1024)(128)(4,1)} %bitcast.66), calls=%async_computation.7 | async-start | bytes 8388608
  293.8 7.2 %copy-start.11 = (bf16[1024,512]{1,0:T(8,128)(2,1)S(1)}, bf16[1024,512]{1,0:T(8,128)(2,1)}, u32[]{:S(2)}) copy-start(bf16[1024,512]{1,0:T(8,128)(2,1)} %convolution_convert_fusion.7) | copy-start | bytes 3145732
  303.7 180.6 %reduce-scatter.5.cloned.1.call-start = ((), (), s32[]{:S(2)}) async-start(), calls=%async_computation.5 | async-start | bytes 8912896 | tf_op jit(solution)/shard_map/reduce_scatter | solution.py:280
  306.7 7.7 %copy-start.8 = (bf16[1024,2048]{1,0:T(8,128)(2,1)}, bf16[1024,2048]{1,0:T(8,128)(2,1)S(1)}, u32[]{:S(2)}) copy-start(bf16[1024,2048]{1,0:T(8,128)(2,1)S(1)} %slice.157) | copy-start | bytes 12582916
  306.8 33.8 %copy-start.15 = (f32[512]{0:T(512)S(1)}, f32[512]{0:T(512)}, u32[]{:S(2)}) copy-start(f32[512]{0:T(512)} %param.28) | copy-start | bytes 6148
  314.5 26.1 %collective-permute-start.4 = (bf16[1184,512]{1,0:T(8,128)(2,1)}, bf16[1184,512]{1,0:T(8,128)(2,1)}, u32[]{:S(2)}, u32[]{:S(2)}) collective-permute-start(bf16[1184,512]{1,0:T(8,128)(2,1)} %convolution_convert_fusion.6), channel_id=1, source_target_pairs={{0,1},{1,0},{2,3},{3,2},{4,5},{5,4},{6,7},{7,6},{8,9},{9,8},{10,11... | collective-permute-start | bytes 3637256 | tf_op jit(solution)/shard_map/ppermute | solution.py:27
  364.7 25.6 %copy-start.12 = (f32[512]{0:T(512)S(1)}, f32[512]{0:T(512)}, u32[]{:S(2)}) copy-start(f32[512]{0:T(512)} %param.17) | copy-start | bytes 6148
  364.7 25.5 %collective-permute-start.6 = (bf16[1184,512]{1,0:T(8,128)(2,1)}, bf16[1184,512]{1,0:T(8,128)(2,1)S(1)}, u32[]{:S(2)}, u32[]{:S(2)}) collective-permute-start(bf16[1184,512]{1,0:T(8,128)(2,1)} %dynamic-slice_convert_fusion), channel_id=1, source_target_pairs={{0,1},{1,0},{2,3},{3,2},{4,5},{5,4},{6,7},{7,6},{8,9},{9,8},{10,11... | collective-permute-start | bytes 3637256 | tf_op jit(solution)/shard_map/ppermute | solution.py:27
  366.2 24.0 %collective-permute-start.7 = (f32[2,1184]{1,0:T(2,128)S(1)}, f32[2,1184]{1,0:T(2,128)S(1)}, u32[]{:S(2)}, u32[]{:S(2)}) collective-permute-start(f32[2,1184]{1,0:T(2,128)S(1)} %pad_maximum_fusion.7), channel_id=1, source_target_pairs={{0,1},{1,0},{2,3},{3,2},{4,5},{5,4},{6,7},{7,6},{8,9},{9,8},{10,11... | collective-permute-start | bytes 28424 | tf_op jit(solution)/shard_map/ppermute | solution.py:27
  (10 other events, 32.4 us)
Sparse Core Ops, SparseCore 0:
  10.7 53.0 all-gather.2
  66.6 72.8 all-gather.4
  303.8 73.0 reduce-scatter.2
  380.8 103.3 reduce-scatter.4
